TPU v7x, 32 devices: a whole 2x2x4 slice. The times are simulated.
32 devices in a mesh: groups: 2 (over x), chan: 16 (over z, y, core).
Axes of the slice: x: 2, y: 2, z: 4, core: 2. Of those that a mesh axis runs over, the one named last changes fastest.
Arguments:
- data: bfloat16 [28672, 4096], P(('groups', 'chan')), parts along dimension 0, as said below
- alive: int32 [8192], P(('groups', 'chan')), parts along dimension 0, may hold values 0 or 1
- sources: int32 [2, 16], replicated, may hold values from 0 to 4095, as said below
Outputs:
- correlations: bfloat16 [4, 16, 256, 4096], P('groups', None, None, 'chan'), parts along dimension 0
There are 2 independent parts, one for each index of `groups`. A program takes and returns all parts, laid end to end along the dimension named above; an argument that names none is the same for every part. Nothing has to cross between parts.
Inputs may be any that keep to these rules, and one draw needn't show every extreme that they name: `sources`: no channel number appears twice in the array, and channel 4096 - 1 is always one of them. `data`: samples have channel and time-block scales of their own.
All inputs are finite; a program needn't handle non-finite values. No bound on the sum of `alive` on one device may be relied on, other than what follows from the above.
Results may differ from a plain program's by a relative error of at most 0.0076.
Values may be sent and summed in bfloat16 or wider, within the bound.
No kernel may reach another device: no remote copies, remote signals or barrier semaphores. Data moves between devices by JAX's collectives and lax.ppermute only.
A program may use at most 128 MiB of HBM per device.

v0:
```python
import math
import jax
import jax.numpy as jnp
from jax import lax
from jax.sharding import PartitionSpec as P

SEGMENT_LENGTH = 512
NF = 128
LAGS = 256
SRC = 16
ROUNDS = 2
SEGMENT_TALLY = 28


def forward_table():
    times = jnp.arange(SEGMENT_LENGTH, dtype=jnp.int32)[:, None]
    bins = jnp.arange(NF, dtype=jnp.int32)[None, :] + 1
    angle = 2.0 * math.pi / SEGMENT_LENGTH * (bins * times % SEGMENT_LENGTH).astype(jnp.float32)
    table = jnp.concatenate([jnp.cos(angle), -jnp.sin(angle)], axis=1) / math.sqrt(SEGMENT_LENGTH)
    return table.astype(jnp.bfloat16)


def inverse_table():
    shifts = jnp.arange(LAGS, dtype=jnp.int32)[:, None] - LAGS // 2
    bins = jnp.arange(NF, dtype=jnp.int32)[None, :] + 1
    angle = 2.0 * math.pi / SEGMENT_LENGTH * (bins * shifts % SEGMENT_LENGTH).astype(jnp.float32)
    return jnp.concatenate([jnp.cos(angle), -jnp.sin(angle)], axis=1).astype(jnp.bfloat16)


def body(data, alive, sources):
    count = lax.axis_size("chan")
    width = data.shape[1] // count
    table = forward_table()
    split = data.reshape(data.shape[0], count, width)
    moved = lax.all_to_all(split, "chan", split_axis=1, concat_axis=0, tiled=True)
    blocks = moved.reshape(SEGMENT_TALLY, SEGMENT_LENGTH, moved.shape[2])
    spectra = jnp.einsum("tk,wtc->wkc", table, blocks, preferred_element_type=jnp.float32)
    level = jnp.mean(spectra[:, :NF] ** 2 + spectra[:, NF:] ** 2, axis=0)
    factor = alive.astype(jnp.float32)[None, :] / jnp.sqrt(level + 0.01)
    factor = jnp.concatenate([factor, factor], axis=0)
    whitened = (spectra * factor[None]).astype(jnp.bfloat16)
    ids = sources.reshape(-1)
    owner = ids // width
    local = ids % width
    mine = owner == lax.axis_index("chan")
    picked = jnp.transpose(jnp.take(whitened, local, axis=2), (2, 0, 1)).astype(jnp.float32)
    picked = jnp.where(mine[:, None, None], picked, 0.0)
    src = lax.psum(picked, "chan").astype(jnp.bfloat16)
    src_re, src_im = (src[:, :, :NF], src[:, :, NF:])
    own_re, own_im = (whitened[:, :NF], whitened[:, NF:])
    form = "qwf,wfc->qfc"
    correlogram_realpart = jnp.einsum(
        form, src_re, own_re, preferred_element_type=jnp.float32
    ) + jnp.einsum(form, src_im, own_im, preferred_element_type=jnp.float32)
    cross_imaginary = jnp.einsum(
        form, src_re, own_im, preferred_element_type=jnp.float32
    ) - jnp.einsum(form, src_im, own_re, preferred_element_type=jnp.float32)
    cross = jnp.concatenate([correlogram_realpart, cross_imaginary], axis=1).astype(jnp.bfloat16)
    lagged = jnp.einsum("lk,qkc->qlc", inverse_table(), cross, preferred_element_type=jnp.float32)
    lagged = lagged / math.sqrt(NF * SEGMENT_TALLY)
    return lagged.reshape(ROUNDS, SRC, LAGS, width).astype(jnp.bfloat16)


def solution(mesh):
    return jax.shard_map(
        body,
        mesh=mesh,
        in_specs=(P(("groups", "chan"), None), P(("groups", "chan")), P()),
        out_specs=P("groups", None, None, "chan"),
        check_vma=False,
    )
```

profile of v0, /device:TPU:0, one launch (start us, length us, event | category | flops | bytes accessed | tf_op | source)
XLA Modules:
  0.0 326.9 jit_solution(7985542122648060904)
XLA Ops:
  0.0 6.9 %copy.27 = bf16[112,16,8,256]{3,2,0,1:T(8,128)(2,1)} copy(bf16[112,16,8,256]{3,2,1,0:T(8,128)(2,1)} %bitcast.32) | data formatting | bytes 14680064 | tf_op jit(solution)/shard_map/reshape | solution.py:34
  6.9 7.6 %all-to-all-start = ((bf16[896,16,256]{2,0,1:T(8,128)(2,1)}), bf16[896,16,256]{2,0,1:T(8,128)(2,1)}, u32[]{:S(2)}, u32[]{:S(2)}) async-start(bf16[896,16,256]{2,0,1:T(8,128)(2,1)} %bitcast.31), calls=%async_computation | async-start | bytes 14680064 | tf_op jit(solution)/shard_map/all_to_all | solution.py:35
  14.7 0.6 cosine_convert_fusion
  15.3 1.1 fusion.33
  16.4 130.5 %all-to-all-done = bf16[896,16,256]{2,0,1:T(8,128)(2,1)} async-done(((bf16[896,16,256]{2,0,1:T(8,128)(2,1)}), bf16[896,16,256]{2,0,1:T(8,128)(2,1)}, u32[]{:S(2)}, u32[]{:S(2)}) %all-to-all-start) | async-done | bytes 7340064 | tf_op jit(solution)/shard_map/all_to_all | solution.py:35
  146.9 5.2 %convolution_bitcast_fusion = f32[28,256,256]{2,1,0:T(8,128)S(1)} fusion(bf16[28,512,256]{2,1,0:T(8,128)(2,1)} %bitcast.3, f32[512,128]{0,1:T(8,128)S(1)} %get-tuple-element.14, f32[512,128]{0,1:T(8,128)S(1)} %get-tuple-element.13), kind=kOutput, calls=%fused_computation.14 | convolution fusion | flops 1879441408 | bytes 15204352 | tf_op jit(solution)/shard_map/tk,wtc->wkc/dot_general | solution.py:37
  152.6 2.6 multiply_convert_fusion.1
  155.2 7.7 %copy.7 = bf16[28,256,256]{1,0,2:T(8,128)(2,1)} copy(bf16[28,256,256]{2,1,0:T(8,128)(2,1)} %multiply_convert_fusion.1) | data formatting | bytes 7340032 | tf_op jit(solution)/shard_map/convert_element_type | solution.py:41
  162.9 3.6 %fusion.40 = (bf16[28,128,256]{2,1,0:T(8,128)(2,1)S(1)}, bf16[28,128,256]{2,1,0:T(8,128)(2,1)}) fusion(bf16[28,256,256]{2,1,0:T(8,128)(2,1)} %multiply_convert_fusion.1), kind=kLoop, calls=%fused_computation.76 | loop fusion | bytes 7340032 | tf_op jit(solution)/shard_map/slice | solution.py:50
  166.6 2.8 gather_fusion
  169.6 100.6 %all-reduce.1 = bf16[32,28,256]{2,1,0:T(8,128)(2,1)S(1)} all-reduce(f32[32,28,256]{2,1,0:T(8,128)S(1)} %convert_select_fusion), channel_id=1, replica_groups=mesh['groups'=2,'chan'=16] {'chan'}, use_global_device_ids=true, to_apply=%region_1.2 | all-reduce | flops 229376 | bytes 1376256 | tf_op jit(solution)/shard_map/psum | solution.py:48
  270.3 2.6 copy.13
  272.8 1.6 copy.10
  274.5 4.6 %fusion.14 = f32[128,256,32]{1,2,0:T(8,128)} fusion(bf16[32,28,128]{0,1,2:T(8,128)(2,1)} %copy.13, bf16[28,128,256]{2,1,0:T(8,128)(2,1)S(1)} %get-tuple-element.5), kind=kOutput, calls=%fused_computation.21 | convolution fusion | flops 58720256 | bytes 6258688 | tf_op jit(solution)/shard_map/qwf,wfc->qfc/dot_general | solution.py:57
  279.1 3.2 fusion.12
  282.4 3.3 fusion.10
  285.6 3.3 %fusion.16 = f32[128,256,32]{1,2,0:T(8,128)} fusion(bf16[32,28,128]{0,1,2:T(8,128)(2,1)S(1)} %copy.10, bf16[28,128,256]{2,1,0:T(8,128)(2,1)S(1)} %get-tuple-element.5), kind=kOutput, calls=%fused_computation.23 | convolution fusion | flops 58720256 | bytes 6258688 | tf_op jit(solution)/shard_map/qwf,wfc->qfc/dot_general | solution.py:52
  288.9 5.3 %copy.16 = f32[128,256,32]{0,1,2:T(8,128)} copy(f32[128,256,32]{1,2,0:T(8,128)} %fusion.14) | data formatting | bytes 8388608 | tf_op jit(solution)/shard_map/qwf,wfc->qfc/dot_general | solution.py:57
  294.2 5.3 %copy.15 = f32[128,256,32]{0,1,2:T(8,128)} copy(f32[128,256,32]{1,2,0:T(8,128)} %fusion.10) | data formatting | bytes 8388608 | tf_op jit(solution)/shard_map/qwf,wfc->qfc/dot_general | solution.py:55
  299.6 5.3 %copy.14 = f32[128,256,32]{0,1,2:T(8,128)} copy(f32[128,256,32]{1,2,0:T(8,128)} %fusion.12) | data formatting | bytes 8388608 | tf_op jit(solution)/shard_map/qwf,wfc->qfc/dot_general | solution.py:54
  304.9 5.3 %copy.11 = f32[128,256,32]{0,1,2:T(8,128)} copy(f32[128,256,32]{1,2,0:T(8,128)} %fusion.16) | data formatting | bytes 8388608 | tf_op jit(solution)/shard_map/qwf,wfc->qfc/dot_general | solution.py:52
  310.2 7.6 %fusion.8 = (bf16[32,128,256]{1,2,0:T(8,128)(2,1)S(1)}, bf16[32,128,256]{1,2,0:T(8,128)(2,1)S(1)}) fusion(f32[128,256,32]{0,1,2:T(8,128)} %copy.11, f32[128,256,32]{0,1,2:T(8,128)} %copy.14, f32[128,256,32]{0,1,2:T(8,128)} %copy.15, f32[128,256,32]{0,1,2:T(8,128)} %copy.16), kind=kLoop, calls=%fused_computation.15 | loop fusion | flops 4194304 | bytes 20971520 | tf_op jit(solution)/shard_map/add | solution.py:52
  317.8 2.9 multiply_convert_fusion
  320.7 6.2 %copy.8 = bf16[2,16,256,256]{3,2,1,0:T(8,128)(2,1)} copy(bf16[2,16,256,256]{2,3,1,0:T(8,128)(2,1)} %bitcast.33) | data formatting | bytes 8388608 | tf_op jit(solution)/shard_map/convert_element_type | solution.py:61
  (21 shorter events, 1.1 us)
Async XLA Ops:
  6.9 7.6 %copy-start.3 = (s32[2,16]{1,0:T(2,128)S(1)}, s32[2,16]{1,0:T(2,128)}, u32[]{:S(2)}) copy-start(s32[2,16]{1,0:T(2,128)} %param.5) | copy-start | bytes 388
  6.9 7.8 %copy-start.2 = (s32[256]{0:T(256)S(1)}, s32[256]{0:T(256)}, u32[]{:S(2)}) copy-start(s32[256]{0:T(256)} %param.4) | copy-start | bytes 3076
  6.9 140.0 %all-to-all-start = ((bf16[896,16,256]{2,0,1:T(8,128)(2,1)}), bf16[896,16,256]{2,0,1:T(8,128)(2,1)}, u32[]{:S(2)}, u32[]{:S(2)}) async-start(bf16[896,16,256]{2,0,1:T(8,128)(2,1)} %bitcast.31), calls=%async_computation | async-start | bytes 14680064 | tf_op jit(solution)/shard_map/all_to_all | solution.py:35
  274.5 4.7 %copy-start = (bf16[28,128,256]{2,1,0:T(8,128)(2,1)S(1)}, bf16[28,128,256]{2,1,0:T(8,128)(2,1)}, u32[]{:S(2)}) copy-start(bf16[28,128,256]{2,1,0:T(8,128)(2,1)} %get-tuple-element.6) | copy-start | bytes 5505028
  274.5 4.7 %copy-start.1 = (bf16[32,28,128]{0,1,2:T(8,128)(2,1)S(1)}, bf16[32,28,128]{0,1,2:T(8,128)(2,1)}, u32[]{:S(2)}) copy-start(bf16[32,28,128]{0,1,2:T(8,128)(2,1)} %copy.13) | copy-start | bytes 688132
where the time goes:
time: 328 us; the launch traced here: 327 us
  waiting for transfers between devices  130 us (40%)
  blocking collectives  101 us (31%)
  local copies, waits for them, and re-layouts  52.9 us (16%)
  matrix products  22.5 us (7%)
  other arithmetic  12.8 us (4%)
  starting transfers between devices  7.56 us (2%)
    all_to_all x1, waiting for transfers between devices, body(): lax.all_to_all(split, 'chan', split_axis=1, concat_axis=0, tiled=True)  130 us
    psum x1, blocking collectives, body(): src = lax.psum(picked, 'chan').astype(jnp.bfloat16)  101 us
    convert_element_type x1, local copies, waits for them, and re-layouts, body(): whitened = (spectra * factor[None]).astype(jnp.bfloat16)  7.7 us
    add x1, other arithmetic, body(): jnp.einsum(form, src_re, own_re, preferred_element_type=jnp.float32)  7.63 us
    all_to_all x1, starting transfers between devices, body(): lax.all_to_all(split, 'chan', split_axis=1, concat_axis=0, tiled=True)  7.56 us
    reshape x1, local copies, waits for them, and re-layouts, body(): split = data.reshape(data.shape[0], count, width)  6.85 us
  transfers between devices with their start and end apart: 1, of which 1 were waited for; matrix products, arithmetic and copies ran while one was open for 1% of the time, Pallas kernels for 0%

commit v1 on v0

--- a/solution.py
+++ b/solution.py
@@ -32,7 +32,10 @@
     width = data.shape[1] // count
     table = forward_table()
     split = data.reshape(data.shape[0], count, width)
-    moved = lax.all_to_all(split, "chan", split_axis=1, concat_axis=0, tiled=True)
+    moved = jnp.concatenate(
+        lax.all_to_all(jnp.stack(jnp.split(split, lax.axis_size("chan"), axis=1)), "chan", 0, 0),
+        axis=0,
+    )
     blocks = moved.reshape(SEGMENT_TALLY, SEGMENT_LENGTH, moved.shape[2])
     spectra = jnp.einsum("tk,wtc->wkc", table, blocks, preferred_element_type=jnp.float32)
     level = jnp.mean(spectra[:, :NF] ** 2 + spectra[:, NF:] ** 2, axis=0)

time: 328 us -> 360 us (1.098)
  blocking collectives: 101 us -> 123 us
  local copies, waits for them, and re-layouts: 52.9 us -> 72.6 us
  other arithmetic: 12.8 us -> 6.3 us
  matrix products: 22.5 us -> 16.9 us
    unnamed x8 -> x26, local copies, waits for them, and re-layouts: 0.02 us -> 32.1 us
    psum x1, blocking collectives: 101 us -> 123 us  [body(): src = lax.psum(picked, 'chan').astype(jnp.bfloat16)]
    dot_general x4 -> x0, local copies, waits for them, and re-layouts: 21.3 us -> none  [the longest x1 5.34 us: body(): jnp.einsum(form, src_re, own_im, preferred_element_type=jnp.float32)]
    all_to_all x0 -> x1, local copies, waits for them, and re-layouts: none -> 11.2 us  [body(): lax.all_to_all(jnp.stack(jnp.split(split, lax.axis_size('chan'), axis=1))...]
    slice x1 -> x3, local copies, waits for them, and re-layouts: 3.64 us -> 11.8 us  [body(): own_re, own_im = (whitened[:, :NF], whitened[:, NF:])]
    add x1 -> x0, other arithmetic: 7.63 us -> none  [body(): jnp.einsum(form, src_re, own_re, preferred_element_type=jnp.float32)]
    reshape x1 -> x0, local copies, waits for them, and re-layouts: 6.85 us -> none  [body(): split = data.reshape(data.shape[0], count, width)]
    dot_general x1, matrix products: 2.88 us -> 7.23 us  [body(): jnp.einsum('lk,qkc->qlc', inverse_table(), cross, preferred_element_type=...]
where the time goes in v1:
time: 360 us; the launch traced here: 357 us
  waiting for transfers between devices  131 us (36%)
  blocking collectives  123 us (34%)
  local copies, waits for them, and re-layouts  72.6 us (20%)
  matrix products  16.9 us (5%)
  starting transfers between devices  7.56 us (2%)
  other arithmetic  6.3 us (2%)
    all_to_all x1, waiting for transfers between devices, body(): lax.all_to_all(jnp.stack(jnp.split(split, lax.axis_size('chan'), axis=1))...  131 us
    psum x1, blocking collectives, body(): src = lax.psum(picked, 'chan').astype(jnp.bfloat16)  123 us
    unnamed x26, local copies, waits for them, and re-layouts  32.1 us
    slice x3, local copies, waits for them, and re-layouts, body(): own_re, own_im = (whitened[:, :NF], whitened[:, NF:])  11.8 us
    all_to_all x1, local copies, waits for them, and re-layouts, body(): lax.all_to_all(jnp.stack(jnp.split(split, lax.axis_size('chan'), axis=1))...  11.2 us
    all_to_all x1, starting transfers between devices, body(): lax.all_to_all(jnp.stack(jnp.split(split, lax.axis_size('chan'), axis=1))...  7.56 us
    dot_general x1, matrix products, body(): jnp.einsum('lk,qkc->qlc', inverse_table(), cross, preferred_element_type=...  7.23 us
  transfers between devices with their start and end apart: 1, of which 1 were waited for; matrix products, arithmetic and copies ran while one was open for 1% of the time, Pallas kernels for 0%

profile of v1, /device:TPU:0, one launch (start us, length us, event | category | flops | bytes accessed | tf_op | source)
XLA Modules:
  0.0 357.0 jit_solution(10420531642395725895)
XLA Ops:
  0.0 10.8 %copy.23 = bf16[896,4096]{0,1:T(8,128)(2,1)} copy(bf16[896,4096]{1,0:T(8,128)(2,1)} %param.3) | data formatting | bytes 14680064 | tf_op args[0]
  10.8 2.0 fusion.30
  12.8 2.3 fusion.29
  15.0 1.9 fusion.28
  16.9 1.9 fusion.27
  18.8 1.8 fusion.26
  20.6 1.8 fusion.25
  22.5 1.8 fusion.24
  24.3 1.9 fusion.23
  32.7 7.6 %all-to-all-start = ((bf16[16,896,1,256]{1,3,2,0:T(8,128)(2,1)}), bf16[16,896,1,256]{1,3,2,0:T(8,128)(2,1)}, u32[]{:S(2)}, u32[]{:S(2)}) async-start(bf16[16,896,1,256]{1,3,2,0:T(8,128)(2,1)} %fusion.15), calls=%async_computation | async-start | bytes 14680064 | tf_op jit(solution)/shard_map/all_to_all | solution.py:36
  42.2 130.5 %all-to-all-done = bf16[16,896,1,256]{1,3,2,0:T(8,128)(2,1)} async-done(((bf16[16,896,1,256]{1,3,2,0:T(8,128)(2,1)}), bf16[16,896,1,256]{1,3,2,0:T(8,128)(2,1)}, u32[]{:S(2)}, u32[]{:S(2)}) %all-to-all-start) | async-done | bytes 7340064 | tf_op jit(solution)/shard_map/all_to_all | solution.py:36
  172.7 11.2 %copy.26 = bf16[16,896,1,256]{3,1,0,2:T(8,128)(2,1)} copy(bf16[16,896,1,256]{1,3,2,0:T(8,128)(2,1)} %all-to-all-done) | data formatting | bytes 14680064 | tf_op jit(solution)/shard_map/all_to_all | solution.py:36
  183.9 5.2 %convolution_bitcast_fusion = f32[28,256,256]{1,2,0:T(8,128)S(1)} fusion(bf16[28,512,256]{2,1,0:T(8,128)(2,1)} %bitcast.88, f32[512,128]{1,0:T(8,128)S(1)} %get-tuple-element.12, f32[512,128]{1,0:T(8,128)S(1)} %get-tuple-element.11), kind=kOutput, calls=%fused_computation.13 | convolution fusion | flops 1879441408 | bytes 15204352 | tf_op jit(solution)/shard_map/tk,wtc->wkc/dot_general | solution.py:40
  190.7 4.2 %copy.28 = bf16[28,256,256]{1,0,2:T(8,128)(2,1)} copy(bf16[28,256,256]{1,2,0:T(8,128)(2,1)S(1)} %multiply_convert_fusion.1) | data formatting | bytes 7340032 | tf_op jit(solution)/shard_map/convert_element_type | solution.py:44
  194.8 2.9 fusion.52
  197.7 2.8 gather_fusion
  200.5 3.4 copy.29
  203.9 2.7 convert_select_fusion
  206.6 122.9 %all-reduce.1 = bf16[32,28,256]{1,0,2:T(8,128)(2,1)S(1)} all-reduce(f32[32,28,256]{1,0,2:T(8,128)} %convert_select_fusion), channel_id=1, replica_groups=mesh['groups'=2,'chan'=16] {'chan'}, use_global_device_ids=true, to_apply=%region_1.2 | all-reduce | flops 229376 | bytes 1376256 | tf_op jit(solution)/shard_map/psum | solution.py:51
  329.5 4.5 %copy.30 = bf16[28,128,256]{2,0,1:T(8,128)(2,1)} copy(bf16[28,128,256]{1,2,0:T(8,128)(2,1)} %get-tuple-element.5) | data formatting | bytes 3670016 | tf_op jit(solution)/shard_map/slice | solution.py:53
  334.0 4.4 %copy.31 = bf16[28,128,256]{2,0,1:T(8,128)(2,1)} copy(bf16[28,128,256]{1,2,0:T(8,128)(2,1)} %get-tuple-element.6) | data formatting | bytes 3670016 | tf_op jit(solution)/shard_map/slice | solution.py:53
  338.4 2.4 fusion.12
  343.5 7.2 %multiply_convert_fusion = bf16[32,256,256]{2,1,0:T(8,128)(2,1)} fusion(bf16[32,256,256]{2,0,1:T(8,128)(2,1)S(1)} %pad_maximum_fusion, bf16[256,128]{1,0:T(8,128)(2,1)S(1)} %get-tuple-element.8, bf16[256,128]{1,0:T(8,128)(2,1)S(1)} %get-tuple-element.7), kind=kOutput, calls=%fused_computation.1 | convolution fusion | flops 1078198272 | bytes 8519680 | tf_op jit(solution)/shard_map/lk,qkc->qlc/dot_general | solution.py:62
  350.8 6.2 %copy.35 = bf16[2,16,256,256]{3,2,1,0:T(8,128)(2,1)} copy(bf16[2,16,256,256]{2,3,1,0:T(8,128)(2,1)} %bitcast.105) | data formatting | bytes 8388608 | tf_op jit(solution)/shard_map/convert_element_type | solution.py:64
  (36 shorter events, 12.6 us)
Async XLA Ops:
  10.8 15.3 %copy-start = (bf16[896,4096]{0,1:T(8,128)(2,1)S(1)}, bf16[896,4096]{0,1:T(8,128)(2,1)}, u32[]{:S(2)}) copy-start(bf16[896,4096]{0,1:T(8,128)(2,1)} %copy.23) | copy-start | bytes 22020100
  32.7 7.6 %copy-start.4 = (s32[2,16]{1,0:T(2,128)S(1)}, s32[2,16]{1,0:T(2,128)}, u32[]{:S(2)}) copy-start(s32[2,16]{1,0:T(2,128)} %param.5) | copy-start | bytes 388
  32.7 7.8 %copy-start.3 = (s32[256]{0:T(256)S(1)}, s32[256]{0:T(256)}, u32[]{:S(2)}) copy-start(s32[256]{0:T(256)} %param.4) | copy-start | bytes 3076
  32.7 140.0 %all-to-all-start = ((bf16[16,896,1,256]{1,3,2,0:T(8,128)(2,1)}), bf16[16,896,1,256]{1,3,2,0:T(8,128)(2,1)}, u32[]{:S(2)}, u32[]{:S(2)}) async-start(bf16[16,896,1,256]{1,3,2,0:T(8,128)(2,1)} %fusion.15), calls=%async_computation | async-start | bytes 14680064 | tf_op jit(solution)/shard_map/all_to_all | solution.py:36
  338.4 2.4 copy-start.2
  340.9 1.6 copy-start.1
